TPU v7x, 32 devices: a whole 2x2x4 slice. The times are simulated.
32 devices in a mesh: band: 8 (over z, y), grid: 4 (over x, core).
Axes of the slice: x: 2, y: 2, z: 4, core: 2. Of those that a mesh axis runs over, the one named last changes fastest.
Arguments:
- bands: bfloat16 [2, 16, 128, 128, 128], P(None, 'band', 'grid'), may hold values from -6 to 6
- occupations: float32 [16], P('band'), may hold values from 0.25 to 1
- external: float32 [128, 128, 128], P('grid'), may hold values from 0 to 2
- density_in: float32 [128, 128, 128], P('grid'), may hold values from -0.2 to 1.4
- prev_density: float32 [128, 128, 128], P('grid'), may hold values from 0 to 1.2
- prev_residual: float32 [128, 128, 128], P('grid'), may hold values from -1.3 to 0.3
- hist_density: float32 [5, 128, 128, 128], P(None, 'grid'), may hold values from 0 to 1
- hist_residual: float32 [5, 128, 128, 128], P(None, 'grid'), may hold values from -0.6 to 1
Outputs:
- density: float32 [128, 128, 128], P('grid')
- residual: float32 [128, 128, 128], P('grid')
All inputs are finite; a program needn't handle non-finite values.
Results may differ from a plain program's by a relative error of at most 0.018.
The roundings to bfloat16 on the way count: a program that leaves them out, or rounds other values in their place, can miss the bound.
Values may be sent and summed in bfloat16 or wider, within the bound.
A program may use at most 192 MiB of HBM per device.

v0:
```python
import math

import jax
import jax.numpy as jnp
from jax import lax
from jax.sharding import PartitionSpec as P

NG = 128
DEPTH = 6
ITERS = 3


time_step = 0.25
energy_shift = 2.5
coupling = 1.0
mixing_weight = 0.5
ridge_share = 0.1
ridge_floor = 0.01
density_scale = 8.0
highest = lax.Precision.HIGHEST


def fourier_tables(length, frequency):
    positions = jnp.arange(length, dtype=jnp.int32)
    phase_index = positions[:, None] * frequency[None, :] % length
    angles = phase_index.astype(jnp.float32) * (2.0 * math.pi / length)
    unit_scale = 1.0 / math.sqrt(length)
    return (
        (jnp.cos(angles) * unit_scale).astype(jnp.bfloat16),
        (jnp.sin(angles) * unit_scale).astype(jnp.bfloat16),
    )


def complex_block(cosine_part, sine_part, orientation):
    sine_signed = sine_part * orientation
    upper_half = jnp.concatenate([cosine_part, sine_signed], axis=1)
    lower_half = jnp.concatenate([-sine_signed, cosine_part], axis=1)
    return jnp.concatenate([upper_half, lower_half], axis=0)


def solve_definite(matrix, vector):
    extent = matrix.shape[0]
    factor_low = jnp.zeros_like(matrix)
    for column in range(extent):
        pivot_value = jnp.sqrt(
            matrix[column, column]
            - jnp.sum(factor_low[column, :column] * factor_low[column, :column])
        )
        factor_low = factor_low.at[column, column].set(pivot_value)
        for row_index in range(column + 1, extent):
            element = (
                matrix[row_index, column]
                - jnp.sum(factor_low[row_index, :column] * factor_low[column, :column])
            ) / pivot_value
            factor_low = factor_low.at[row_index, column].set(element)
    middle = jnp.zeros_like(vector)
    for row_index in range(extent):
        element = (
            vector[row_index] - jnp.sum(factor_low[row_index, :row_index] * middle[:row_index])
        ) / factor_low[row_index, row_index]
        middle = middle.at[row_index].set(element)
    result = jnp.zeros_like(vector)
    for row_index in reversed(range(extent)):
        element = (
            middle[row_index]
            - jnp.sum(factor_low[row_index + 1 :, row_index] * result[row_index + 1 :])
        ) / factor_low[row_index, row_index]
        result = result.at[row_index].set(element)
    return result


def local(
    bands,
    occupations,
    external,
    density_in,
    prev_density,
    prev_residual,
    hist_density,
    hist_residual,
):
    grid_count = lax.axis_size("grid")
    band_count = lax.axis_size("band")
    slab_planes = external.shape[0]
    cells_total = NG * NG * NG
    bands_total = occupations.shape[0] * band_count
    frequency = jnp.arange(-(NG // 4), NG // 4, dtype=jnp.int32)
    kept_count = frequency.shape[0]
    inside = ((frequency >= -(NG // 4)) & (frequency < NG // 4)).astype(jnp.float32)
    cosine_part, sine_part = fourier_tables(NG, frequency)
    forward_block = complex_block(cosine_part, sine_part, -1.0)
    inverse_block = complex_block(cosine_part.T, sine_part.T, 1.0)
    forward_axis = forward_block.reshape(2, NG, 2, kept_count)
    inverse_axis = inverse_block.reshape(2, kept_count, 2, NG)
    column_rows = kept_count // grid_count
    column_start = lax.axis_index("grid") * column_rows
    local_freq = lax.dynamic_slice_in_dim(frequency, column_start, column_rows).astype(jnp.float32)
    local_inside = lax.dynamic_slice_in_dim(inside, column_start, column_rows)
    squared = frequency.astype(jnp.float32) * frequency.astype(jnp.float32)
    quarter = NG / 4.0
    radius = (
        squared[None, :, None] + (local_freq * local_freq)[:, None, None] + squared[None, None, :]
    )
    kinetic = jnp.exp(-time_step * radius / (quarter * quarter))
    kinetic = kinetic * local_inside[:, None, None] * inside[None, :, None] * inside[None, None, :]
    history_flat = hist_residual.reshape(DEPTH - 1, -1)
    gram_kept = lax.psum(
        jnp.dot(history_flat, history_flat.T, precision=highest) / cells_total, "grid"
    )
    orbitals = jnp.concatenate([bands[0], bands[1]], axis=-1)
    density_now = density_in
    density_prev = prev_density
    residual_prev = prev_residual
    density_diffs = hist_density
    residual_diffs = hist_residual
    residual = density_in
    for iteration in range(ITERS):
        factor = jnp.exp(-time_step * (external + coupling * density_now - energy_shift))
        doubled = jnp.concatenate([factor, factor], axis=-1)
        weighted = (orbitals.astype(jnp.float32) * doubled).astype(jnp.bfloat16)
        band_items = orbitals.shape[0]
        along_z = jnp.dot(weighted, forward_block, preferred_element_type=jnp.float32).astype(
            jnp.bfloat16
        )
        split_z = along_z.reshape(band_items, slab_planes, NG, 2, kept_count)
        along_y = jnp.einsum(
            "bxycz,cydk->bkxdz", split_z, forward_axis, preferred_element_type=jnp.float32
        )
        along_y = along_y.astype(jnp.bfloat16).reshape(
            band_items, kept_count, slab_planes, 2 * kept_count
        )
        exchanged = lax.all_to_all(along_y, "grid", split_axis=1, concat_axis=2, tiled=True)
        item_count = exchanged.shape[0]
        spread = exchanged.reshape(item_count, column_rows, NG, 2, kept_count)
        spectral = jnp.einsum(
            "byxcz,cxdk->bykdz", spread, forward_axis, preferred_element_type=jnp.float32
        )
        damped = (spectral * kinetic[None, :, :, None, :]).astype(jnp.bfloat16)
        spatial = jnp.einsum(
            "bykdz,dkcx->byxcz", damped, inverse_axis, preferred_element_type=jnp.float32
        )
        returned = lax.all_to_all(
            spatial.astype(jnp.bfloat16).reshape(item_count, column_rows, NG, 2 * kept_count),
            "grid",
            split_axis=2,
            concat_axis=1,
            tiled=True,
        )
        split_back = returned.reshape(band_items, kept_count, slab_planes, 2, kept_count)
        back_y = jnp.einsum(
            "bkxdz,dkcy->bxycz", split_back, inverse_axis, preferred_element_type=jnp.float32
        )
        back_y = back_y.astype(jnp.bfloat16).reshape(band_items, slab_planes, NG, 2 * kept_count)
        orbitals = jnp.dot(back_y, inverse_block, preferred_element_type=jnp.float32).astype(
            jnp.bfloat16
        )
        real_part = orbitals[..., :NG].astype(jnp.float32)
        imag_part = orbitals[..., NG:].astype(jnp.float32)
        weighted_sq = occupations[:, None, None, None] * (
            real_part * real_part + imag_part * imag_part
        )
        density_out = lax.psum(
            (jnp.sum(weighted_sq, axis=0) * (density_scale / bands_total)).astype(jnp.bfloat16),
            "band",
        ).astype(jnp.float32)
        mixing_density_diffs = density_diffs
        mixing_residual_diffs = residual_diffs
        mixing_residual = density_out - density_now
        newest = mixing_residual - residual_prev
        mixing_density_diffs = jnp.concatenate(
            [
                mixing_density_diffs[mixing_density_diffs.shape[0] - (DEPTH - 1) :],
                (density_now - density_prev)[None],
            ],
            axis=0,
        )
        mixing_residual_diffs = jnp.concatenate(
            [mixing_residual_diffs[mixing_residual_diffs.shape[0] - (DEPTH - 1) :], newest[None]],
            axis=0,
        )
        flat_diffs = mixing_residual_diffs.reshape(DEPTH, -1)
        border_local = jnp.dot(flat_diffs, newest.reshape(-1), precision=highest) / cells_total
        right_local = (
            jnp.dot(flat_diffs, mixing_residual.reshape(-1), precision=highest) / cells_total
        )
        border, right_side = lax.psum((border_local, right_local), "grid")
        gram_matrix = (
            jnp.zeros((DEPTH, DEPTH), jnp.float32).at[: DEPTH - 1, : DEPTH - 1].set(gram_kept)
        )
        gram_matrix = gram_matrix.at[DEPTH - 1, :].set(border).at[:, DEPTH - 1].set(border)
        ridge_value = ridge_share * jnp.trace(gram_matrix) / DEPTH + ridge_floor
        coeffs = solve_definite(
            gram_matrix + ridge_value * jnp.eye(DEPTH, dtype=jnp.float32), right_side
        )
        combined = mixing_density_diffs + mixing_weight * mixing_residual_diffs
        density_next = (
            density_now
            + mixing_weight * mixing_residual
            - jnp.einsum("j,jxyz->xyz", coeffs, combined, precision=highest)
        )
        density_next, residual, density_diffs, residual_diffs, gram_kept = (
            density_next,
            mixing_residual,
            mixing_density_diffs,
            mixing_residual_diffs,
            gram_matrix[1:, 1:],
        )
        density_prev = density_now
        residual_prev = residual
        density_now = density_next
    return (density_now, residual)


def solution(mesh):
    placed = (
        P(None, "band", "grid", None, None),
        P("band"),
        P("grid", None, None),
        P("grid", None, None),
        P("grid", None, None),
        P("grid", None, None),
        P(None, "grid", None, None),
        P(None, "grid", None, None),
    )
    return jax.shard_map(
        local,
        mesh=mesh,
        in_specs=placed,
        out_specs=(P("grid", None, None), P("grid", None, None)),
        check_vma=False,
    )
```

profile of v0, /device:TPU:0, one launch (start us, length us, event | category | flops | bytes accessed | tf_op | source)
XLA Modules:
  0.0 1105.6 jit_solution(15028615402567349357)
XLA Ops:
  7.6 4.1 slice_bitcast_fusion.1
  12.2 2.3 pad_maximum_fusion.5
  14.5 4.4 fusion.49
  20.1 2.2 copy.177
  22.3 1.8 reshape.2946
  24.1 4.2 all-to-all-start
  29.3 13.4 %all-to-all-done = bf16[2,64,32,128]{3,2,0,1:T(8,128)(2,1)S(1)} async-done(((bf16[2,64,32,128]{3,2,0,1:T(8,128)(2,1)}), bf16[2,64,32,128]{3,2,0,1:T(8,128)(2,1)S(1)}, u32[]{:S(2)}, u32[]{:S(2)}) %all-to-all-start) | async-done | bytes 1048608 | tf_op jit(solution)/shard_map/all_to_all | solution.py:132
  43.9 3.9 reshape.2819
  47.7 1.8 fusion.77
  51.8 28.3 %all_to_all.90 = bf16[2,16,128,128]{3,1,0,2:T(8,128)(2,1)S(1)} all-to-all(bf16[2,16,128,128]{3,1,0,2:T(8,128)(2,1)S(1)} %copy.65), channel_id=1, replica_groups=mesh['band'=8,'grid'=4] {'grid'}, dimensions={2} | all-to-all | bytes 2097152 | tf_op jit(solution)/shard_map/all_to_all | solution.py:142
  81.5 3.9 reshape.2821
  85.4 4.3 copy.69
  89.7 2.3 fusion.51
  96.8 54.3 %fusion.83 = f32[5,5]{1,0:T(8,128)S(1)} fusion(f32[5,32,128,128]{3,2,1,0:T(8,128)} %param.231), kind=kOutput, calls=%fused_computation.118 | convolution fusion | flops 157286432 | bytes 10485860 | tf_op jit(solution)/shard_map/dot_general | solution.py:108
  151.1 25.1 %all-reduce.19.cloned.1.call-done = bf16[32,128,128]{2,1,0:T(8,128)(2,1)} async-done(((bf16[32,128,128]{2,1,0:T(8,128)(2,1)}), bf16[32,128,128]{2,1,0:T(8,128)(2,1)}) %all-reduce.19.cloned.1.call-update) | async-done | bytes 1048592 | tf_op jit(solution)/shard_map/psum | solution.py:162
  176.2 3.9 fusion.188
  180.1 13.4 %pad_maximum_fusion = (f32[6,32,128,128]{3,2,1,0:T(8,128)S(1)}, f32[6,32,128,128]{3,2,1,0:T(8,128)}) fusion(f32[1,32,128,128]{3,2,1,0:T(8,128)S(1)} %bitcast.527, f32[5,32,128,128]{3,2,1,0:T(8,128)} %param.231, f32[1,32,128,128]{3,2,1,0:T(8,128)S(1)} %get-tuple-element.1331, f32[5,32,128,128]{3,2,1,0:T(8,128)} %param.230), kind=kLoop, calls=%fused_computation.13 | loop fusion | flops 12582912 | bytes 50331648 | tf_op jit(solution)/shard_map/concatenate | solution.py:177
  193.5 43.1 %fusion.119 = f32[6]{0:T(128)S(1)} fusion(f32[32,128,128,1]{2,3,1,0:T(1,128)S(1)} %bitcast.531, f32[6,32,128,128]{3,2,1,0:T(8,128)S(1)} %get-tuple-element.1325), kind=kOutput, calls=%fused_computation.130 | convolution fusion | flops 37748744 | bytes 14680088 | tf_op jit(solution)/shard_map/dot_general | solution.py:184
  236.6 42.8 %fusion.116 = f32[6]{0:T(128)S(1)} fusion(f32[32,128,128,1]{2,3,1,0:T(1,128)S(1)} %bitcast.528, f32[6,32,128,128]{3,2,1,0:T(8,128)S(1)} %get-tuple-element.1325), kind=kOutput, calls=%fused_computation.129 | convolution fusion | flops 37748744 | bytes 14680088 | tf_op jit(solution)/shard_map/dot_general | solution.py:182
  279.5 6.9 all-reduce.14
  353.1 28.1 %fusion.16 = f32[1,32,128,128]{3,0,2,1:T(1,128)S(1)} fusion(f32[6,32,128,128]{3,2,1,0:T(8,128)} %get-tuple-element.1326, f32[6]{0:T(128)S(1)} %constant_dynamic-update-slice_fusion.26), kind=kOutput, calls=%fused_computation.24 | convolution fusion | flops 37748736 | bytes 14680088 | tf_op jit(solution)/shard_map/j,jxyz->xyz/dot_general | solution.py:199
  381.2 2.4 multiply_exponential_fusion.1
  383.9 1.8 copy-done.5
  388.6 3.5 copy.190
  392.1 4.7 reshape.2947
  396.9 17.9 %all_to_all.91 = bf16[2,64,32,128]{3,2,0,1:T(8,128)(2,1)S(1)} all-to-all(bf16[2,64,32,128]{3,2,0,1:T(8,128)(2,1)} %reshape.2947), channel_id=1, replica_groups=mesh['band'=8,'grid'=4] {'grid'}, dimensions={1} | all-to-all | bytes 2097152 | tf_op jit(solution)/shard_map/all_to_all | solution.py:132
  415.9 5.0 reshape.2843
  420.9 3.4 fusion.78
  424.3 2.3 copy.83
  426.6 2.7 copy.84
  429.2 18.1 %all_to_all.92 = bf16[2,16,128,128]{3,1,0,2:T(8,128)(2,1)S(1)} all-to-all(bf16[2,16,128,128]{3,1,0,2:T(8,128)(2,1)} %copy.84), channel_id=1, replica_groups=mesh['band'=8,'grid'=4] {'grid'}, dimensions={2} | all-to-all | bytes 2097152 | tf_op jit(solution)/shard_map/all_to_all | solution.py:142
  448.7 5.0 reshape.2845
  453.8 6.5 copy.88
  460.3 2.3 fusion.55
  467.5 15.0 %fusion.24 = (f32[5,32,128,128]{3,2,1,0:T(8,128)}, f32[5,32,128,128]{3,2,1,0:T(8,128)}) fusion(f32[5,32,128,128]{3,2,1,0:T(8,128)} %param.230, f32[1,32,128,128]{3,2,1,0:T(8,128)} %copy-done.14, f32[1,32,128,128]{3,2,1,0:T(8,128)S(1)} %bitcast.529, f32[5,32,128,128]{3,2,1,0:T(8,128)} %param.231), kind=kLoop, calls=%fused_computation.38 | loop fusion | flops 5242880 | bytes 46137344 | tf_op jit(solution)/shard_map/concatenate | solution.py:170
  482.5 61.3 %all-reduce.21.cloned.1.call-done = bf16[32,128,128]{2,1,0:T(8,128)(2,1)} async-done(((bf16[32,128,128]{2,1,0:T(8,128)(2,1)}), bf16[32,128,128]{2,1,0:T(8,128)(2,1)}) %all-reduce.21.cloned.1.call-update) | async-done | bytes 1048592 | tf_op jit(solution)/shard_map/psum | solution.py:162
  543.8 4.0 fusion.187
  547.9 4.3 copy-done
  552.2 9.3 pad_maximum_fusion.2
  561.5 43.1 %fusion.113 = f32[6]{0:T(128)S(1)} fusion(f32[32,128,128,1]{2,3,1,0:T(1,128)S(1)} %bitcast.530, f32[6,32,128,128]{3,2,1,0:T(8,128)S(1)} %get-tuple-element.1323), kind=kOutput, calls=%fused_computation.128 | convolution fusion | flops 37748744 | bytes 14680088 | tf_op jit(solution)/shard_map/dot_general | solution.py:184
  604.6 42.9 %fusion.110 = f32[6]{0:T(128)S(1)} fusion(f32[32,128,128,1]{2,3,1,0:T(1,128)S(1)} %bitcast.533, f32[6,32,128,128]{3,2,1,0:T(8,128)S(1)} %get-tuple-element.1323), kind=kOutput, calls=%fused_computation.127 | convolution fusion | flops 37748744 | bytes 14680088 | tf_op jit(solution)/shard_map/dot_general | solution.py:182
  647.4 6.5 all-reduce.13
  721.3 28.1 %fusion.14 = f32[1,32,128,128]{3,0,2,1:T(1,128)S(1)} fusion(f32[6,32,128,128]{3,2,1,0:T(8,128)} %get-tuple-element.1324, f32[6]{0:T(128)S(1)} %constant_dynamic-update-slice_fusion.25), kind=kOutput, calls=%fused_computation.22 | convolution fusion | flops 37748736 | bytes 14680088 | tf_op jit(solution)/shard_map/j,jxyz->xyz/dot_general | solution.py:199
  749.4 2.4 multiply_exponential_fusion
  752.2 1.8 copy-done.3
  756.8 2.2 copy.203
  759.0 1.9 reshape.2948
  760.8 17.9 %all_to_all.93 = bf16[2,64,32,128]{3,2,0,1:T(8,128)(2,1)S(1)} all-to-all(bf16[2,64,32,128]{3,2,0,1:T(8,128)(2,1)} %reshape.2948), channel_id=1, replica_groups=mesh['band'=8,'grid'=4] {'grid'}, dimensions={1} | all-to-all | bytes 2097152 | tf_op jit(solution)/shard_map/all_to_all | solution.py:132
  780.0 3.9 reshape.2867
  783.8 1.9 fusion.79
  788.0 16.9 %all_to_all.94 = bf16[2,16,128,128]{3,1,0,2:T(8,128)(2,1)S(1)} all-to-all(bf16[2,16,128,128]{3,1,0,2:T(8,128)(2,1)S(1)} %copy.101), channel_id=1, replica_groups=mesh['band'=8,'grid'=4] {'grid'}, dimensions={2} | all-to-all | bytes 2097152 | tf_op jit(solution)/shard_map/all_to_all | solution.py:142
  805.3 1.8 reshape.2869
  807.1 5.3 copy.105
  817.0 9.8 fusion.23
  826.8 4.8 fusion.22
  831.6 61.9 %all-reduce.23.cloned.1.call-done = bf16[32,128,128]{2,1,0:T(8,128)(2,1)} async-done(((bf16[32,128,128]{2,1,0:T(8,128)(2,1)}), bf16[32,128,128]{2,1,0:T(8,128)(2,1)}) %all-reduce.23.cloned.1.call-update) | async-done | bytes 1048592 | tf_op jit(solution)/shard_map/psum | solution.py:162
  893.5 4.0 fusion.186
  897.5 2.9 copy-done.1
  900.4 9.4 pad_maximum_fusion.4
  909.8 43.1 %fusion.107 = f32[6]{0:T(128)S(1)} fusion(f32[32,128,128,1]{2,3,1,0:T(1,128)S(1)} %bitcast.537, f32[6,32,128,128]{3,2,1,0:T(8,128)S(1)} %get-tuple-element.1321), kind=kOutput, calls=%fused_computation.126 | convolution fusion | flops 37748744 | bytes 14680088 | tf_op jit(solution)/shard_map/dot_general | solution.py:184
  952.9 42.9 %fusion.104 = f32[6]{0:T(128)S(1)} fusion(f32[32,128,128,1]{2,3,1,0:T(1,128)S(1)} %bitcast.536, f32[6,32,128,128]{3,2,1,0:T(8,128)S(1)} %get-tuple-element.1321), kind=kOutput, calls=%fused_computation.125 | convolution fusion | flops 37748744 | bytes 14680088 | tf_op jit(solution)/shard_map/dot_general | solution.py:182
  995.8 6.5 all-reduce.12
  1069.1 27.6 %fusion.12 = f32[1,32,128,128]{3,0,2,1:T(1,128)S(1)} fusion(f32[6,32,128,128]{3,2,1,0:T(8,128)} %get-tuple-element.1322, f32[6]{0:T(128)S(1)} %constant_dynamic-update-slice_fusion.24), kind=kOutput, calls=%fused_computation.20 | convolution fusion | flops 37748736 | bytes 14680088 | tf_op jit(solution)/shard_map/j,jxyz->xyz/dot_general | solution.py:199
  1096.8 1.9 add_subtract_fusion
  (305 shorter events, 98.2 us)
Async XLA Ops:
  7.6 4.2 copy-start.10
  7.6 4.2 copy-start.15
  24.1 18.7 %all-to-all-start = ((bf16[2,64,32,128]{3,2,0,1:T(8,128)(2,1)}), bf16[2,64,32,128]{3,2,0,1:T(8,128)(2,1)S(1)}, u32[]{:S(2)}, u32[]{:S(2)}) async-start(bf16[2,64,32,128]{3,2,0,1:T(8,128)(2,1)} %reshape.2946), calls=%async_computation | async-start | bytes 2097152 | tf_op jit(solution)/shard_map/all_to_all | solution.py:132
  28.3 147.9 %all-reduce.19.cloned.1.call-start = ((), (), s32[]{:S(2)}) async-start(), calls=%async_computation.6 | async-start | bytes 2097152 | tf_op jit(solution)/shard_map/psum | solution.py:162
  92.2 1.3 copy-start.21
  93.6 1.9 copy-start.4
  96.7 447.1 %all-reduce.21.cloned.1.call-start = ((), (), s32[]{:S(2)}) async-start(), calls=%async_computation.7 | async-start | bytes 2097152 | tf_op jit(solution)/shard_map/psum | solution.py:162
  180.1 13.4 %copy-start.14 = (f32[1,32,128,128]{3,2,1,0:T(8,128)}, f32[1,32,128,128]{3,2,1,0:T(8,128)S(1)}, u32[]{:S(2)}) copy-start(f32[1,32,128,128]{3,2,1,0:T(8,128)S(1)} %get-tuple-element.1331) | copy-start | bytes 6291460
  180.1 13.4 %copy-start.7 = (f32[32,128,128]{2,1,0:T(8,128)}, f32[32,128,128]{2,1,0:T(8,128)S(1)}, u32[]{:S(2)}) copy-start(f32[32,128,128]{2,1,0:T(8,128)S(1)} %get-tuple-element.1320) | copy-start | bytes 6291460
  353.0 28.1 %copy-start.8 = (f32[32,128,128]{2,1,0:T(8,128)S(1)}, f32[32,128,128]{2,1,0:T(8,128)}, u32[]{:S(2)}) copy-start(f32[32,128,128]{2,1,0:T(8,128)} %copy-done.7) | copy-start | bytes 6291460
  353.0 28.1 %copy-start.11 = (f32[32,128,128]{2,1,0:T(8,128)S(1)}, f32[32,128,128]{2,1,0:T(8,128)}, u32[]{:S(2)}) copy-start(f32[32,128,128]{2,1,0:T(8,128)} %param.227) | copy-start | bytes 6291460
  353.1 28.1 %copy-start.16 = (f32[32,128,128]{2,1,0:T(8,128)S(1)}, f32[32,128,128]{2,1,0:T(8,128)}, u32[]{:S(2)}) copy-start(f32[32,128,128]{2,1,0:T(8,128)} %param.226) | copy-start | bytes 6291460
  383.6 2.2 copy-start.5
  464.1 2.0 copy-start.2
  467.4 426.1 %all-reduce.23.cloned.1.call-start = ((), (), s32[]{:S(2)}) async-start(), calls=%async_computation.8 | async-start | bytes 2097152 | tf_op jit(solution)/shard_map/psum | solution.py:162
  543.8 8.4 copy-start
  547.8 13.7 %copy-start.19 = (f32[1,32,128,128]{3,2,1,0:T(8,128)}, f32[1,32,128,128]{3,2,1,0:T(8,128)S(1)}, u32[]{:S(2)}) copy-start(f32[1,32,128,128]{3,2,1,0:T(8,128)S(1)} %get-tuple-element.1330) | copy-start | bytes 6291460
  547.8 56.7 %copy-start.9 = (f32[32,128,128]{2,1,0:T(8,128)}, f32[32,128,128]{2,1,0:T(8,128)S(1)}, u32[]{:S(2)}) copy-start(f32[32,128,128]{2,1,0:T(8,128)S(1)} %get-tuple-element.1315) | copy-start | bytes 6291460
  547.9 201.5 %copy-start.6 = (f32[32,128,128]{2,1,0:T(8,128)}, f32[32,128,128]{2,1,0:T(8,128)S(1)}, u32[]{:S(2)}) copy-start(f32[32,128,128]{2,1,0:T(8,128)S(1)} %get-tuple-element.1316) | copy-start | bytes 6291460
  721.2 28.1 %copy-start.12 = (f32[32,128,128]{2,1,0:T(8,128)S(1)}, f32[32,128,128]{2,1,0:T(8,128)}, u32[]{:S(2)}) copy-start(f32[32,128,128]{2,1,0:T(8,128)} %get-tuple-element.1318) | copy-start | bytes 6291460
  721.2 28.1 %copy-start.17 = (f32[32,128,128]{2,1,0:T(8,128)S(1)}, f32[32,128,128]{2,1,0:T(8,128)}, u32[]{:S(2)}) copy-start(f32[32,128,128]{2,1,0:T(8,128)} %param.226) | copy-start | bytes 6291460
  751.8 2.2 copy-start.3
  815.6 11.2 %slice-start = ((s8[10485760]{0:T(1024)(128)(4,1)}), s8[2097152]{0:T(1024)(128)(4,1)S(1)}, s32[]{:S(2)}) async-start(s8[10485760]{0:T(1024)(128)(4,1)} %bitcast.525), calls=%async_computation.9 | async-start | bytes 4194304
  817.0 9.8 slice-start.1
  817.0 9.8 slice-start.2
  817.0 9.8 copy-start.20
  893.5 6.9 copy-start.1
  897.5 199.2 %copy-start.13 = (f32[32,128,128]{2,1,0:T(8,128)}, f32[32,128,128]{2,1,0:T(8,128)S(1)}, u32[]{:S(2)}) copy-start(f32[32,128,128]{2,1,0:T(8,128)S(1)} %get-tuple-element.1312) | copy-start | bytes 6291460
  1069.1 27.7 %copy-start.18 = (f32[32,128,128]{2,1,0:T(8,128)S(1)}, f32[32,128,128]{2,1,0:T(8,128)}, u32[]{:S(2)}) copy-start(f32[32,128,128]{2,1,0:T(8,128)} %get-tuple-element.1314) | copy-start | bytes 6291460
Sparse Core Ops, SparseCore 0:
  96.9 79.3 all-reduce.18
  467.5 76.2 all-reduce.20
  817.0 76.4 all-reduce.22
where the time goes:
time: 1110 us
  matrix products  423 us (38%)
  waiting for transfers between devices  162 us (15%)
  between operations  152 us (14%)
  other arithmetic  126 us (11%)
  local copies, waits for them, and re-layouts  119 us (11%)
  blocking collectives  119 us (11%)
    psum x3, waiting for transfers between devices, local(): lax.psum((jnp.sum(weighted_sq, axis=0) * (density_scale / bands_total)).a...  148 us
    dot_general x3, matrix products, local(): jnp.dot(flat_diffs, mixing_residual.reshape(-1), precision=highest)  129 us
    dot_general x3, matrix products, local(): jnp.dot(flat_diffs, newest.reshape(-1), precision=highest) / cells_total  129 us
    dot_general x3, matrix products, local(): jnp.einsum('j,jxyz->xyz', coeffs, combined, precision=highest)  83.8 us
    all_to_all x3, blocking collectives, local(): lax.all_to_all(spatial.astype(jnp.bfloat16).reshape(item_count, column_ro...  63.3 us
    dot_general x1, matrix products, local(): jnp.dot(history_flat, history_flat.T, precision=highest) / cells_total  54.3 us
    concatenate x4, other arithmetic, local(): jnp.concatenate([mixing_residual_diffs[mixing_residual_diffs.shape[0] - (...  41.9 us
    all_to_all x2, blocking collectives, local(): lax.all_to_all(along_y, 'grid', split_axis=1, concat_axis=2, tiled=True)  35.8 us
  transfers between devices with their start and end apart: 4, of which 4 were waited for; matrix products, arithmetic and copies ran while one was open for 8% of the time, Pallas kernels for 0%

commit v1 on v0

--- a/solution.py
+++ b/solution.py
@@ -3,6 +3,8 @@
 import jax
 import jax.numpy as jnp
 from jax import lax
+from jax.experimental import pallas as pl
+from jax.experimental.pallas import tpu as pltpu
 from jax.sharding import PartitionSpec as P
 
 NG = 128
@@ -38,35 +40,125 @@
     return jnp.concatenate([upper_half, lower_half], axis=0)
 
 
-def solve_definite(matrix, vector):
-    extent = matrix.shape[0]
-    factor_low = jnp.zeros_like(matrix)
-    for column in range(extent):
-        pivot_value = jnp.sqrt(
-            matrix[column, column]
-            - jnp.sum(factor_low[column, :column] * factor_low[column, :column])
-        )
-        factor_low = factor_low.at[column, column].set(pivot_value)
-        for row_index in range(column + 1, extent):
-            element = (
-                matrix[row_index, column]
-                - jnp.sum(factor_low[row_index, :column] * factor_low[column, :column])
-            ) / pivot_value
-            factor_low = factor_low.at[row_index, column].set(element)
-    middle = jnp.zeros_like(vector)
-    for row_index in range(extent):
-        element = (
-            vector[row_index] - jnp.sum(factor_low[row_index, :row_index] * middle[:row_index])
-        ) / factor_low[row_index, row_index]
-        middle = middle.at[row_index].set(element)
-    result = jnp.zeros_like(vector)
-    for row_index in reversed(range(extent)):
-        element = (
-            middle[row_index]
-            - jnp.sum(factor_low[row_index + 1 :, row_index] * result[row_index + 1 :])
-        ) / factor_low[row_index, row_index]
-        result = result.at[row_index].set(element)
-    return result
+def fold(cells):
+    return jnp.sum(cells.reshape(-1, 8, cells.shape[-1]), axis=0)
+
+
+def gram_kernel(hist_ref, out_ref):
+    @pl.when(pl.program_id(0) == 0)
+    def _():
+        out_ref[...] = jnp.zeros_like(out_ref)
+
+    count = hist_ref.shape[0]
+    for plane in range(hist_ref.shape[1]):
+        entries = [hist_ref[j, plane] for j in range(count)]
+        place = 0
+        for j in range(count):
+            for k in range(j + 1):
+                out_ref[place] += fold(entries[j] * entries[k])
+                place += 1
+
+
+def kept_products(hist):
+    count, planes, rows, lanes = hist.shape
+    pairs = count * (count + 1) // 2
+    return pl.pallas_call(
+        gram_kernel,
+        grid=(planes // 2,),
+        in_specs=[pl.BlockSpec((count, 2, rows, lanes), lambda i: (0, i, 0, 0))],
+        out_specs=pl.BlockSpec((pairs, 8, lanes), lambda i: (0, 0, 0)),
+        out_shape=jax.ShapeDtypeStruct((pairs, 8, lanes), jnp.float32),
+        compiler_params=pltpu.CompilerParams(dimension_semantics=("arbitrary",)),
+    )(hist)
+
+
+def sums_kernel(first, fresh_count, *refs):
+    hist_ref = refs[0]
+    fresh = refs[1 : 1 + fresh_count]
+    total_ref, now_ref, before_ref, residual_ref, newest_ref, out_ref = refs[1 + fresh_count :]
+
+    @pl.when(pl.program_id(0) == 0)
+    def _():
+        out_ref[...] = jnp.zeros_like(out_ref)
+
+    for plane in range(hist_ref.shape[1]):
+        residual = total_ref[plane].astype(jnp.float32) - now_ref[plane]
+        newest = residual - before_ref[plane]
+        residual_ref[plane] = residual
+        newest_ref[plane] = newest
+        entries = [hist_ref[j, plane] for j in range(first, hist_ref.shape[0])]
+        entries += [ref[plane] for ref in fresh] + [newest]
+        for j, entry in enumerate(entries):
+            out_ref[j] += fold(entry * newest)
+            out_ref[len(entries) + j] += fold(entry * residual)
+
+
+def residual_sums(first, hist, fresh, total, now, before):
+    count, planes, rows, lanes = hist.shape
+    cell = pl.BlockSpec((2, rows, lanes), lambda i: (i, 0, 0))
+    field = jax.ShapeDtypeStruct((planes, rows, lanes), jnp.float32)
+    entries = count - first + len(fresh) + 1
+    return pl.pallas_call(
+        lambda *refs: sums_kernel(first, len(fresh), *refs),
+        grid=(planes // 2,),
+        in_specs=[pl.BlockSpec((count, 2, rows, lanes), lambda i: (0, i, 0, 0))]
+        + [cell] * (len(fresh) + 3),
+        out_specs=(cell, cell, pl.BlockSpec((2 * entries, 8, lanes), lambda i: (0, 0, 0))),
+        out_shape=(field, field, jax.ShapeDtypeStruct((2 * entries, 8, lanes), jnp.float32)),
+        compiler_params=pltpu.CompilerParams(dimension_semantics=("arbitrary",)),
+    )(hist, *fresh, total, now, before)
+
+
+def solve_kernel(kept_ref, sums_ref, coeffs_ref, next_ref):
+    last = DEPTH - 1
+    shape = (8, coeffs_ref.shape[1])
+
+    def spot(j, k):
+        return j * (j + 1) // 2 + k
+
+    values = {}
+    for j in range(DEPTH):
+        for k in range(j + 1):
+            values[j, k] = sums_ref[k] if j == last else kept_ref[spot(j, k)]
+    for j in range(last):
+        for k in range(j + 1):
+            next_ref[spot(j, k)] = values[j + 1, k + 1]
+    trace = values[0, 0]
+    for j in range(1, DEPTH):
+        trace = trace + values[j, j]
+    ridge = trace * (ridge_share / DEPTH) + ridge_floor
+    matrix = {}
+    for (j, k), value in values.items():
+        matrix[j, k] = jnp.full(shape, value + ridge if j == k else value, jnp.float32)
+    vector = [jnp.full(shape, sums_ref[DEPTH + j], jnp.float32) for j in range(DEPTH)]
+    inverse = []
+    for k in range(DEPTH):
+        inverse.append(1.0 / matrix[k, k])
+        scaled = {j: matrix[j, k] * inverse[k] for j in range(k + 1, DEPTH)}
+        for j in range(k + 1, DEPTH):
+            vector[j] = vector[j] - scaled[j] * vector[k]
+            for m in range(k + 1, j + 1):
+                matrix[j, m] = matrix[j, m] - scaled[j] * matrix[m, k]
+    for k in reversed(range(DEPTH)):
+        value = vector[k]
+        for j in range(k + 1, DEPTH):
+            value = value - matrix[j, k] * vector[j]
+        vector[k] = value * inverse[k]
+    for k in range(DEPTH):
+        coeffs_ref[pl.ds(k, 1), :] = vector[k][:1]
+
+
+def solve_definite(kept, sums, lanes):
+    scalars = pl.BlockSpec(memory_space=pltpu.SMEM)
+    return pl.pallas_call(
+        solve_kernel,
+        in_specs=[scalars, scalars],
+        out_specs=(pl.BlockSpec(memory_space=pltpu.VMEM), scalars),
+        out_shape=(
+            jax.ShapeDtypeStruct((DEPTH, lanes), jnp.float32),
+            jax.ShapeDtypeStruct(kept.shape, jnp.float32),
+        ),
+    )(kept, sums)
 
 
 def local(
@@ -103,16 +195,16 @@
     )
     kinetic = jnp.exp(-time_step * radius / (quarter * quarter))
     kinetic = kinetic * local_inside[:, None, None] * inside[None, :, None] * inside[None, None, :]
-    history_flat = hist_residual.reshape(DEPTH - 1, -1)
     gram_kept = lax.psum(
-        jnp.dot(history_flat, history_flat.T, precision=highest) / cells_total, "grid"
+        jnp.sum(kept_products(hist_residual), axis=(1, 2)) / cells_total, "grid"
     )
     orbitals = jnp.concatenate([bands[0], bands[1]], axis=-1)
     density_now = density_in
     density_prev = prev_density
     residual_prev = prev_residual
-    density_diffs = hist_density
-    residual_diffs = hist_residual
+    density_diffs = [hist_density[j] for j in range(DEPTH - 1)]
+    residual_diffs = [hist_residual[j] for j in range(DEPTH - 1)]
+    fresh = []
     residual = density_in
     for iteration in range(ITERS):
         factor = jnp.exp(-time_step * (external + coupling * density_now - energy_shift))
@@ -162,49 +254,19 @@
         density_out = lax.psum(
             (jnp.sum(weighted_sq, axis=0) * (density_scale / bands_total)).astype(jnp.bfloat16),
             "band",
-        ).astype(jnp.float32)
-        mixing_density_diffs = density_diffs
-        mixing_residual_diffs = residual_diffs
-        mixing_residual = density_out - density_now
-        newest = mixing_residual - residual_prev
-        mixing_density_diffs = jnp.concatenate(
-            [
-                mixing_density_diffs[mixing_density_diffs.shape[0] - (DEPTH - 1) :],
-                (density_now - density_prev)[None],
-            ],
-            axis=0,
-        )
-        mixing_residual_diffs = jnp.concatenate(
-            [mixing_residual_diffs[mixing_residual_diffs.shape[0] - (DEPTH - 1) :], newest[None]],
-            axis=0,
-        )
-        flat_diffs = mixing_residual_diffs.reshape(DEPTH, -1)
-        border_local = jnp.dot(flat_diffs, newest.reshape(-1), precision=highest) / cells_total
-        right_local = (
-            jnp.dot(flat_diffs, mixing_residual.reshape(-1), precision=highest) / cells_total
-        )
-        border, right_side = lax.psum((border_local, right_local), "grid")
-        gram_matrix = (
-            jnp.zeros((DEPTH, DEPTH), jnp.float32).at[: DEPTH - 1, : DEPTH - 1].set(gram_kept)
-        )
-        gram_matrix = gram_matrix.at[DEPTH - 1, :].set(border).at[:, DEPTH - 1].set(border)
-        ridge_value = ridge_share * jnp.trace(gram_matrix) / DEPTH + ridge_floor
-        coeffs = solve_definite(
-            gram_matrix + ridge_value * jnp.eye(DEPTH, dtype=jnp.float32), right_side
-        )
-        combined = mixing_density_diffs + mixing_weight * mixing_residual_diffs
-        density_next = (
-            density_now
-            + mixing_weight * mixing_residual
-            - jnp.einsum("j,jxyz->xyz", coeffs, combined, precision=highest)
-        )
-        density_next, residual, density_diffs, residual_diffs, gram_kept = (
-            density_next,
-            mixing_residual,
-            mixing_density_diffs,
-            mixing_residual_diffs,
-            gram_matrix[1:, 1:],
-        )
+        )
+        residual, newest, partial = residual_sums(
+            iteration, hist_residual, fresh, density_out, density_now, residual_prev
+        )
+        fresh = fresh + [newest]
+        density_diffs = density_diffs[-(DEPTH - 1) :] + [density_now - density_prev]
+        residual_diffs = residual_diffs[-(DEPTH - 1) :] + [newest]
+        sums = lax.psum(jnp.sum(partial, axis=(1, 2)) / cells_total, "grid")
+        coeffs, gram_kept = solve_definite(gram_kept, sums, NG)
+        density_next = density_now + mixing_weight * residual
+        for j in range(DEPTH):
+            combined = density_diffs[j] + mixing_weight * residual_diffs[j]
+            density_next = density_next - coeffs[j][None, None, :] * combined
         density_prev = density_now
         residual_prev = residual
         density_now = density_next

time: 1110 us -> 598 us (0.54)
  matrix products: 423 us -> 28 us
  between operations: 152 us -> 14.4 us
  other arithmetic: 126 us -> 52.7 us
  waiting for transfers between devices: 162 us -> 234 us
  Pallas kernels: 0 us -> 54 us
  local copies, waits for them, and re-layouts: 119 us -> 90.4 us
    dot_general x10 -> x0, matrix products: 396 us -> none  [the longest x3 129 us: local(): jnp.dot(flat_diffs, mixing_residual.reshape(-1), precision=highest)]
    psum x3, waiting for transfers between devices: 148 us -> 221 us  [local(): lax.psum((jnp.sum(weighted_sq, axis=0) * (density_scale / bands_total)).a...]
    concatenate x6 -> x0, other arithmetic: 61.7 us -> none  [the longest x4 41.9 us: local(): jnp.concatenate([mixing_residual_diffs[mixing_residual_diffs.shape[0] - (...]
    pallas_call x0 -> x7, Pallas kernels: none -> 54 us  [the longest x3 38.8 us: residual_sums(): pl.pallas_call(lambda *refs: sums_kernel(first, len(fresh), *refs), grid=...]
    reduce_sum x54 -> x4, other arithmetic: 34.6 us -> 3.92 us  [the longest x3 2.9 us: local(): sums = lax.psum(jnp.sum(partial, axis=(1, 2)) / cells_total, 'grid')]
    exp x3, other arithmetic: 5.23 us -> 28 us  [local(): jnp.exp(-time_step * (external + coupling * density_now - energy_shift))]
    slice x44 -> x0, local copies, waits for them, and re-layouts: 20.7 us -> none  [the longest x12 7.03 us: solve_definite(): factor_low[column, :column]]
  transfers between devices with their start and end apart: 4 -> 4, of which waited for: 4 -> 4; matrix products, arithmetic and copies ran while one was open for 8% -> 0% of each run, Pallas kernels for 0% -> 2%
where the time goes in v1:
time: 598 us; the launch traced here: 588 us
  waiting for transfers between devices  234 us (39%)
  blocking collectives  110 us (18%)
  local copies, waits for them, and re-layouts  90.4 us (15%)
  Pallas kernels  54 us (9%)
  other arithmetic  52.7 us (9%)
  matrix products  28 us (5%)
  between operations  14.4 us (2%)
    psum x3, waiting for transfers between devices, local(): lax.psum((jnp.sum(weighted_sq, axis=0) * (density_scale / bands_total)).a...  221 us
    all_to_all x3, blocking collectives, local(): lax.all_to_all(spatial.astype(jnp.bfloat16).reshape(item_count, column_ro...  53.2 us
    pallas_call x3, Pallas kernels, residual_sums(): pl.pallas_call(lambda *refs: sums_kernel(first, len(fresh), *refs), grid=...  38.8 us
    all_to_all x2, blocking collectives, local(): lax.all_to_all(along_y, 'grid', split_axis=1, concat_axis=2, tiled=True)  35.8 us
    reshape x6, local copies, waits for them, and re-layouts, local(): returned.reshape(band_items, kept_count, slab_planes, 2, kept_count)  28 us
    exp x3, other arithmetic, local(): jnp.exp(-time_step * (external + coupling * density_now - energy_shift))  28 us
    reshape x6, local copies, waits for them, and re-layouts, local(): along_y.astype(jnp.bfloat16)  20.4 us
    psum x2, blocking collectives, local(): sums = lax.psum(jnp.sum(partial, axis=(1, 2)) / cells_total, 'grid')  14 us
  transfers between devices with their start and end apart: 4, of which 4 were waited for; matrix products, arithmetic and copies ran while one was open for 0% of the time, Pallas kernels for 2%

profile of v1, /device:TPU:0, one launch (start us, length us, event | category | flops | bytes accessed | tf_op | source)
XLA Modules:
  0.0 588.4 jit_solution(4792244395911128288)
XLA Ops:
  7.6 2.7 multiply_exponential_fusion.2
  10.7 1.8 copy-done.5
  13.1 1.8 fusion.41
  14.9 1.2 fusion.42
  16.1 2.2 copy.137
  18.3 1.8 reshape.233
  20.0 4.2 all-to-all-start
  25.3 13.5 %all-to-all-done = bf16[2,64,32,128]{3,2,0,1:T(8,128)(2,1)S(1)} async-done(((bf16[2,64,32,128]{3,2,0,1:T(8,128)(2,1)}), bf16[2,64,32,128]{3,2,0,1:T(8,128)(2,1)S(1)}, u32[]{:S(2)}, u32[]{:S(2)}) %all-to-all-start) | async-done | bytes 1048608 | tf_op jit(solution)/shard_map/all_to_all | solution.py:224
  39.8 3.9 reshape.179
  43.7 1.8 fusion.69
  45.5 1.3 copy.54
  47.8 17.0 %all_to_all.90 = bf16[2,16,128,128]{3,1,0,2:T(8,128)(2,1)S(1)} all-to-all(bf16[2,16,128,128]{3,1,0,2:T(8,128)(2,1)S(1)} %copy.55), channel_id=1, replica_groups=mesh['band'=8,'grid'=4] {'grid'}, dimensions={2} | all-to-all | bytes 2097152 | tf_op jit(solution)/shard_map/all_to_all | solution.py:234
  64.8 1.4 copy.57
  66.2 3.9 reshape.181
  70.0 4.3 copy.59
  74.3 2.3 fusion.43
  76.9 1.3 convolution_convert_fusion.2
  81.4 11.1 %shard_map.96 = f32[15,8,128]{2,1,0:T(8,128)} custom-call(f32[5,32,128,128]{3,2,1,0:T(8,128)} %refs_0_.5), custom_call_target="tpu_custom_call" | custom-call | tf_op jit(solution)/shard_map/pallas_call | solution.py:65
  93.5 67.4 %all-reduce.5.cloned.1.call-done.refs_1_ = bf16[32,128,128]{2,1,0:T(8,128)(2,1)} async-done(((bf16[32,128,128]{2,1,0:T(8,128)(2,1)}), bf16[32,128,128]{2,1,0:T(8,128)(2,1)}) %all-reduce.5.cloned.1.call-update) | async-done | bytes 1048592 | tf_op jit(solution)/shard_map/psum | solution.py:254
  160.9 12.6 %shard_map.95 = (f32[32,128,128]{2,1,0:T(8,128)}, f32[32,128,128]{2,1,0:T(8,128)}, f32[12,8,128]{2,1,0:T(8,128)}) custom-call(f32[5,32,128,128]{3,2,1,0:T(8,128)} %refs_0_.5, bf16[32,128,128]{2,1,0:T(8,128)(2,1)} %all-reduce.5.cloned.1.call-done.refs_1_, f32[32,128,128]{2,1,0:T(8,128)} %refs_2_.1, f32[32,128,128]{2,1,0:T(8,128)} %refs_3_.1), custom_call_target="tpu_custom_call" | custom-call | tf_op jit(solution)/shard_map/pallas_call | solution.py:101
  174.5 7.4 %all-reduce = (f32[15]{0:T(128)}, f32[12]{0:T(128)}) all-reduce(f32[15]{0:T(128)S(1)} %broadcast_multiply_fusion.3, f32[12]{0:T(128)S(1)} %broadcast_multiply_fusion.2), channel_id=1, replica_groups=mesh['band'=8,'grid'=4] {'grid'}, use_global_device_ids=true, to_apply=%region_3.4 | all-reduce | flops 27 | bytes 216 | tf_op jit(solution)/shard_map/psum | solution.py:198
  181.9 1.4 shard_map.97
  184.2 12.6 %multiply_exponential_fusion.1 = (f32[32,128,128]{2,1,0:T(8,128)S(1)}, f32[32,128,128]{2,1,0:T(8,128)}) fusion(f32[32,128,128]{2,1,0:T(8,128)} %param.10, f32[32,128,128]{2,1,0:T(8,128)} %get-tuple-element.19.refs_1_, f32[32,128,128]{2,1,0:T(8,128)S(1)} %copy-done, f32[32,128,128]{2,1,0:T(8,128)} %param.12, f32[128]{0:T(128)S(1)} %get-tuple-element.51, ...), kind=kLoop, calls=%fused_computation.79 | loop fusion | flops 15728640 | bytes 35654656 | tf_op jit(solution)/shard_map/exp | solution.py:210
  197.2 1.8 copy-done.2
  199.0 1.6 fusion.40
  200.6 1.2 fusion.46
  201.9 3.5 copy.150
  205.3 4.8 reshape.234
  210.1 17.9 %all_to_all.91 = bf16[2,64,32,128]{3,2,0,1:T(8,128)(2,1)S(1)} all-to-all(bf16[2,64,32,128]{3,2,0,1:T(8,128)(2,1)} %reshape.234), channel_id=1, replica_groups=mesh['band'=8,'grid'=4] {'grid'}, dimensions={1} | all-to-all | bytes 2097152 | tf_op jit(solution)/shard_map/all_to_all | solution.py:224
  229.1 5.0 reshape.185
  234.1 3.4 fusion.70
  237.5 2.3 copy.70
  239.8 2.7 copy.71
  242.4 18.1 %all_to_all.92 = bf16[2,16,128,128]{3,1,0,2:T(8,128)(2,1)S(1)} all-to-all(bf16[2,16,128,128]{3,1,0,2:T(8,128)(2,1)} %copy.71), channel_id=1, replica_groups=mesh['band'=8,'grid'=4] {'grid'}, dimensions={2} | all-to-all | bytes 2097152 | tf_op jit(solution)/shard_map/all_to_all | solution.py:234
  260.5 1.4 copy.73
  261.9 5.0 reshape.187
  266.9 6.5 %copy.75 = bf16[2,64,32,2,64]{1,4,3,2,0:T(8,128)(2,1)} copy(bf16[2,64,32,2,64]{4,3,2,1,0:T(2,128)(2,1)} %reshape.187) | data formatting | bytes 2097152 | tf_op jit(solution)/shard_map/reshape | solution.py:241
  273.4 2.3 fusion.47
  276.0 1.3 convolution_convert_fusion.1
  280.5 76.6 %all-reduce.7.cloned.1.call-done.refs_2_ = bf16[32,128,128]{2,1,0:T(8,128)(2,1)} async-done(((bf16[32,128,128]{2,1,0:T(8,128)(2,1)}), bf16[32,128,128]{2,1,0:T(8,128)(2,1)}) %all-reduce.7.cloned.1.call-update) | async-done | bytes 1048592 | tf_op jit(solution)/shard_map/psum | solution.py:254
  357.0 13.0 %shard_map.98 = (f32[32,128,128]{2,1,0:T(8,128)}, f32[32,128,128]{2,1,0:T(8,128)}, f32[12,8,128]{2,1,0:T(8,128)}) custom-call(f32[5,32,128,128]{3,2,1,0:T(8,128)} %refs_0_.5, f32[32,128,128]{2,1,0:T(8,128)} %get-tuple-element.19.refs_1_, bf16[32,128,128]{2,1,0:T(8,128)(2,1)} %all-reduce.7.cloned.1.call-done.refs_2_, ...), custom_call_target="tpu_custom_call" | custom-call | tf_op jit(solution)/shard_map/pallas_call | solution.py:101
  371.0 7.0 %psum.53.sums_ref = f32[12]{0:T(128)} all-reduce(f32[12]{0:T(128)S(1)} %broadcast_multiply_fusion.1), channel_id=1, replica_groups=mesh['band'=8,'grid'=4] {'grid'}, use_global_device_ids=true, to_apply=%region_9.10 | all-reduce | flops 12 | bytes 96 | tf_op jit(solution)/shard_map/psum | solution.py:264
  378.0 1.4 shard_map.99
  380.3 12.6 %multiply_exponential_fusion = (f32[32,128,128]{2,1,0:T(8,128)S(1)}, f32[32,128,128]{2,1,0:T(8,128)}) fusion(f32[32,128,128]{2,1,0:T(8,128)} %param.10, f32[32,128,128]{2,1,0:T(8,128)} %get-tuple-element.24.refs_2_, f32[32,128,128]{2,1,0:T(8,128)} %get-tuple-element.35.refs_3_, f32[32,128,128]{2,1,0:T(8,128)S(1)} %copy-done, f32[128]{0:T(128)S(1)} %get-tuple-element.45, ...), kind=kLoop, calls=%fused_computation.76 | loop fusion | flops 16252928 | bytes 35654656 | tf_op jit(solution)/shard_map/exp | solution.py:210
  393.3 1.8 copy-done.4
  395.1 1.6 fusion.39
  396.7 1.2 fusion.50
  397.9 3.5 copy.163
  401.4 4.8 reshape.235
  406.2 17.9 %all_to_all.93 = bf16[2,64,32,128]{3,2,0,1:T(8,128)(2,1)S(1)} all-to-all(bf16[2,64,32,128]{3,2,0,1:T(8,128)(2,1)} %reshape.235), channel_id=1, replica_groups=mesh['band'=8,'grid'=4] {'grid'}, dimensions={1} | all-to-all | bytes 2097152 | tf_op jit(solution)/shard_map/all_to_all | solution.py:224
  425.2 5.0 reshape.191
  430.2 3.4 fusion.71
  433.6 1.3 copy.86
  434.9 1.7 copy.87
  436.5 18.1 %all_to_all.94 = bf16[2,16,128,128]{3,1,0,2:T(8,128)(2,1)S(1)} all-to-all(bf16[2,16,128,128]{3,1,0,2:T(8,128)(2,1)} %copy.87), channel_id=1, replica_groups=mesh['band'=8,'grid'=4] {'grid'}, dimensions={2} | all-to-all | bytes 2097152 | tf_op jit(solution)/shard_map/all_to_all | solution.py:234
  455.1 1.8 reshape.193
  456.9 6.5 %copy.91 = bf16[2,64,32,2,64]{1,4,3,2,0:T(8,128)(2,1)} copy(bf16[2,64,32,2,64]{4,3,2,1,0:T(2,128)(2,1)} %reshape.193) | data formatting | bytes 2097152 | tf_op jit(solution)/shard_map/reshape | solution.py:241
  463.4 2.3 fusion.51
  466.0 1.3 convolution_convert_fusion
  469.5 76.6 %all-reduce.9.cloned.1.call-done.refs_3_ = bf16[32,128,128]{2,1,0:T(8,128)(2,1)} async-done(((bf16[32,128,128]{2,1,0:T(8,128)(2,1)}), bf16[32,128,128]{2,1,0:T(8,128)(2,1)}) %all-reduce.9.cloned.1.call-update) | async-done | bytes 1048592 | tf_op jit(solution)/shard_map/psum | solution.py:254
  546.1 13.3 %shard_map.100 = (f32[32,128,128]{2,1,0:T(8,128)}, f32[32,128,128]{2,1,0:T(8,128)}, f32[12,8,128]{2,1,0:T(8,128)}) custom-call(f32[5,32,128,128]{3,2,1,0:T(8,128)} %refs_0_.5, f32[32,128,128]{2,1,0:T(8,128)} %get-tuple-element.19.refs_1_, f32[32,128,128]{2,1,0:T(8,128)} %get-tuple-element.24.refs_2_, ...), custom_call_target="tpu_custom_call" | custom-call | tf_op jit(solution)/shard_map/pallas_call | solution.py:101
  560.4 7.0 %psum.55.sums_ref = f32[12]{0:T(128)} all-reduce(f32[12]{0:T(128)S(1)} %broadcast_multiply_fusion), channel_id=1, replica_groups=mesh['band'=8,'grid'=4] {'grid'}, use_global_device_ids=true, to_apply=%region_13.14 | all-reduce | flops 12 | bytes 96 | tf_op jit(solution)/shard_map/psum | solution.py:264
  567.4 1.4 shard_map.101
  569.7 11.9 %fusion.26 = f32[32,128,128]{2,1,0:T(8,128)} fusion(f32[32,128,128]{2,1,0:T(8,128)} %get-tuple-element.29, f32[32,128,128]{2,1,0:T(8,128)} %get-tuple-element.33.refs_4_, f32[32,128,128]{2,1,0:T(8,128)} %get-tuple-element.35.refs_3_, f32[32,128,128]{2,1,0:T(8,128)} %get-tuple-element.15, f32[128]{0:T(128)S(1)} %get-tuple-element.39, ...), kind=kLoop, calls=%fused_computation.52 | loop fusion | flops 15204352 | bytes 31460352 | tf_op jit(solution)/shard_map/sub | solution.py:269
  (61 shorter events, 23.7 us)
Async XLA Ops:
  10.3 2.2 copy-start.5
  20.0 18.7 %all-to-all-start = ((bf16[2,64,32,128]{3,2,0,1:T(8,128)(2,1)}), bf16[2,64,32,128]{3,2,0,1:T(8,128)(2,1)S(1)}, u32[]{:S(2)}, u32[]{:S(2)}) async-start(bf16[2,64,32,128]{3,2,0,1:T(8,128)(2,1)} %reshape.233), calls=%async_computation | async-start | bytes 2097152 | tf_op jit(solution)/shard_map/all_to_all | solution.py:224
  24.3 136.7 %all-reduce.5.cloned.1.call-start = ((), (), s32[]{:S(2)}) async-start(), calls=%async_computation.6 | async-start | bytes 2097152 | tf_op jit(solution)/shard_map/psum | solution.py:254
  76.9 1.3 copy-start.6
  78.2 1.9 copy-start.1
  81.4 275.7 %all-reduce.7.cloned.1.call-start = ((), (), s32[]{:S(2)}) async-start(), calls=%async_computation.7 | async-start | bytes 2097152 | tf_op jit(solution)/shard_map/psum | solution.py:254
  93.5 90.7 %copy-start = (f32[32,128,128]{2,1,0:T(8,128)S(1)}, f32[32,128,128]{2,1,0:T(8,128)}, u32[]{:S(2)}) copy-start(f32[32,128,128]{2,1,0:T(8,128)} %refs_2_.1) | copy-start | bytes 6291460
  196.9 2.2 copy-start.2
  277.3 1.9 copy-start.3
  280.4 265.7 %all-reduce.9.cloned.1.call-start = ((), (), s32[]{:S(2)}) async-start(), calls=%async_computation.8 | async-start | bytes 2097152 | tf_op jit(solution)/shard_map/psum | solution.py:254
  392.9 2.2 copy-start.4
Sparse Core Ops, SparseCore 0:
  81.5 79.3 all-reduce.4
  280.6 76.4 all-reduce.6
  469.6 76.4 all-reduce.8
